TPU v7x, 32 devices: a whole 2x2x4 slice. The times are simulated.
32 devices in a mesh: head: 2 (over y), view: 4 (over z), row: 4 (over x, core).
Axes of the slice: x: 2, y: 2, z: 4, core: 2. Of those that a mesh axis runs over, the one named last changes fastest.
Arguments:
- query_feats: bfloat16 [4, 32, 16, 1024], P('view', 'row', None, 'head'), may hold values from -125 to 125
- key_feats: bfloat16 [4, 32, 16, 1024], P('view', 'row', None, 'head'), may hold values from -7 to 7
- value_feats: bfloat16 [4, 32, 16, 1024], P('view', 'row', None, 'head'), may hold values from -6 to 6
- target: bfloat16 [4, 32, 16, 1024], P('view', 'row', None, 'head'), may hold values from -6 to 6
- token_rates: float32 [4, 2, 512], P('view', 'head', 'row'), may hold values from 5 to 100
- row_reach: int32 [32], P('row'), may hold values from 1 to 2
- view_counts: int32 [4], P('view'), may hold values from 170 to 512
- w_first: bfloat16 [2, 512, 512], P('head'), may hold values from -0.25 to 0.25
- w_third: bfloat16 [2, 512, 512], P('head'), may hold values from -0.25 to 0.25
- w_second: bfloat16 [2, 512, 512], P('head'), may hold values from -0.25 to 0.25
Outputs:
- fast_out: bfloat16 [4, 32, 16, 1024], P('view', 'row', None, 'head')
All inputs are finite; a program needn't handle non-finite values.
Results may differ from a plain program's by a relative error of at most 0.03.
Values may be sent and summed in bfloat16 or wider, within the bound.
A program may use at most 64 MiB of HBM per device.

v0:
```python
import math

import jax
import jax.numpy as jnp
from jax import lax
from jax.sharding import PartitionSpec as P

HD = 512
ATT_HD = 128
HALO = 2


def with_halo(value, sides, width):
    for axis, dim in sides:
        size, length = (lax.axis_size(axis), value.shape[dim])
        up = [(i, (i + 1) % size) for i in range(size - 1)]
        down = [(j, i) for i, j in up]
        last = lax.slice_in_dim(value, length - width, length, axis=dim)
        leading = lax.slice_in_dim(value, 0, width, axis=dim)
        before = lax.ppermute(last, axis, up)
        after = lax.ppermute(leading, axis, down)
        value = jnp.concatenate([before, value, after], axis=dim)
    return value


def silu_slope(values_in):
    sigmoid_x = jax.nn.sigmoid(values_in)
    return sigmoid_x * (1.0 + values_in * (1.0 - sigmoid_x))


def attend(
    query_rows,
    key_rows,
    value_rows,
    q_row_ids,
    k_row_ids,
    q_tok,
    k_tok,
    k_valid,
    q_reach,
    grid_rows,
):
    count_q = query_rows.shape[0]
    count_k = key_rows.shape[0]
    groups = query_rows.shape[1] // ATT_HD
    query_heads = query_rows.reshape(count_q, groups, ATT_HD)
    key_heads = key_rows.reshape(count_k, groups, ATT_HD)
    value_heads = value_rows.reshape(count_k, groups, ATT_HD)
    scores = jnp.einsum(
        "qhd,khd->hqk", query_heads, key_heads, preferred_element_type=jnp.float32
    ) / math.sqrt(ATT_HD)
    inside = (k_row_ids >= 0) & (k_row_ids < grid_rows)
    in_band = jnp.abs(k_row_ids[None, :] - q_row_ids[:, None]) <= q_reach[:, None]
    allowed = in_band & inside[None, :] & (k_valid[None, :] | (k_tok[None, :] == q_tok[:, None]))
    scores = jnp.where(allowed[None], scores, -1e30)
    row_top = jnp.max(scores, -1, keepdims=True)
    powers = jnp.exp(scores - row_top)
    weights = (powers / jnp.sum(powers, -1, keepdims=True)).astype(jnp.bfloat16)
    output_rows = jnp.einsum(
        "hqk,khd->qhd", weights, value_heads, preferred_element_type=jnp.float32
    )
    return output_rows.reshape(count_q, groups * ATT_HD).astype(jnp.bfloat16)


def renorm(old_matrix, grad, total_valid):
    old_rows = old_matrix.astype(jnp.float32)
    raised = old_rows + grad / total_valid
    rescale = jnp.sqrt(jnp.sum(old_rows * old_rows, -1, keepdims=True) + 1e-06) / jnp.sqrt(
        jnp.sum(raised * raised, -1, keepdims=True) + 1e-06
    )
    return (raised * rescale).astype(jnp.bfloat16)


def per_device(
    query_feats,
    key_feats,
    value_feats,
    target,
    token_rates,
    row_reach,
    view_counts,
    w_first,
    w_third,
    w_second,
):
    row_count = query_feats.shape[1]
    col_count = query_feats.shape[2]
    feat_width = query_feats.shape[3]
    heads_here = feat_width // HD
    tokens_here = row_count * col_count
    key_span = row_count + 2 * HALO
    grid_rows = lax.axis_size("row") * row_count
    row_base = lax.axis_index("row") * row_count
    view_total = view_counts[0]
    total_valid = lax.psum(view_total.astype(jnp.float32), "view")
    paired = jnp.stack([key_feats[0], value_feats[0]], 0)
    padded = with_halo(paired, (("row", 1),), HALO)
    q_row_ids = row_base + jnp.repeat(jnp.arange(row_count, dtype=jnp.int32), col_count)
    k_row_ids = row_base - HALO + jnp.repeat(jnp.arange(key_span, dtype=jnp.int32), col_count)
    q_tok = q_row_ids * col_count + jnp.tile(jnp.arange(col_count, dtype=jnp.int32), row_count)
    k_tok = k_row_ids * col_count + jnp.tile(jnp.arange(col_count, dtype=jnp.int32), key_span)
    k_valid = k_tok < view_total
    q_reach = jnp.repeat(row_reach, col_count)
    attended = attend(
        query_feats[0].reshape(tokens_here, feat_width),
        padded[0].reshape(key_span * col_count, feat_width),
        padded[1].reshape(key_span * col_count, feat_width),
        q_row_ids,
        k_row_ids,
        q_tok,
        k_tok,
        k_valid,
        q_reach,
        grid_rows,
    )
    attended = attended.reshape(tokens_here, heads_here, HD).astype(jnp.float32)
    fast_keys = (
        attended * lax.rsqrt(jnp.mean(attended * attended, -1, keepdims=True) + 1e-06)
    ).astype(jnp.bfloat16)
    valid_mask = (q_tok < view_total).astype(jnp.float32)
    rates_tok = token_rates[0].T
    scaled = (
        rates_tok[:, :, None]
        * valid_mask[:, None, None]
        * target[0].reshape(tokens_here, heads_here, HD).astype(jnp.float32)
    ).astype(jnp.bfloat16)
    first_proj = jnp.einsum("thi,hij->thj", fast_keys, w_first, preferred_element_type=jnp.float32)
    third_proj = jnp.einsum("thi,hij->thj", fast_keys, w_third, preferred_element_type=jnp.float32)
    gated_rows = (jax.nn.silu(first_proj) * third_proj).astype(jnp.bfloat16)
    back_rows = jnp.einsum("tho,hjo->thj", scaled, w_second, preferred_element_type=jnp.float32)
    back_first = (back_rows * third_proj * silu_slope(first_proj)).astype(jnp.bfloat16)
    back_third = (back_rows * jax.nn.silu(first_proj)).astype(jnp.bfloat16)
    grad_first = jnp.einsum(
        "thi,thj->hij", fast_keys, back_first, preferred_element_type=jnp.float32
    )
    grad_third = jnp.einsum(
        "thi,thj->hij", fast_keys, back_third, preferred_element_type=jnp.float32
    )
    grad_second = jnp.einsum("thj,tho->hjo", gated_rows, scaled, preferred_element_type=jnp.float32)
    grad_first, grad_third, grad_second = lax.psum(
        (grad_first, grad_third, grad_second), ("view", "row")
    )
    new_first = renorm(w_first, grad_first, total_valid)
    new_third = renorm(w_third, grad_third, total_valid)
    new_second = renorm(w_second, grad_second, total_valid)
    applied = (
        jax.nn.silu(
            jnp.einsum("thi,hij->thj", fast_keys, new_first, preferred_element_type=jnp.float32)
        )
        * jnp.einsum("thi,hij->thj", fast_keys, new_third, preferred_element_type=jnp.float32)
    ).astype(jnp.bfloat16)
    fast_out = jnp.einsum(
        "thj,hjo->tho", applied, new_second, preferred_element_type=jnp.float32
    ).astype(jnp.bfloat16)
    return fast_out.reshape(1, row_count, col_count, feat_width)


def solution(mesh):
    placed = (
        P("view", "row", None, "head"),
        P("view", "row", None, "head"),
        P("view", "row", None, "head"),
        P("view", "row", None, "head"),
        P("view", "head", "row"),
        P("row"),
        P("view"),
        P("head", None, None),
        P("head", None, None),
        P("head", None, None),
    )
    return jax.shard_map(
        per_device,
        mesh=mesh,
        in_specs=placed,
        out_specs=P("view", "row", None, "head"),
        check_vma=False,
    )
```

profile of v0, /device:TPU:0, one launch (start us, length us, event | category | flops | bytes accessed | tf_op | source)
XLA Modules:
  0.0 147.1 jit_solution(10476243526896424316)
XLA Ops:
  6.5 0.0 copy-start.7
  6.5 0.0 copy-start.2
  6.5 0.0 all-reduce.3.cloned.1.call-start
  6.5 1.0 constant_dynamic-update-slice_fusion.1
  7.5 0.0 copy-done.7
  7.6 0.0 copy-start.6
  7.6 2.4 %collective-permute-start = (bf16[2,2,16,512]{3,2,1,0:T(8,128)(2,1)S(1)}, bf16[2,2,16,512]{3,2,1,0:T(8,128)(2,1)S(1)}, u32[]{:S(2)}, u32[]{:S(2)}) collective-permute-start(bf16[2,2,16,512]{3,2,1,0:T(8,128)(2,1)S(1)} %get-tuple-element.20), channel_id=1, source_target_pairs={{0,1},{1,2},{2,3},{4,5},{5,6},{6,7},{8,9},{9,10},{10,11},{12,13},{... | collective-permute-start | bytes 196616 | tf_op jit(solution)/shard_map/ppermute | solution.py:20
  10.0 1.3 collective-permute-start.1
  12.0 0.0 copy-start.9
  12.0 0.1 add.157
  12.1 0.6 copy-done.9
  12.6 0.1 broadcast_in_dim.20
  12.7 0.1 le.14
  12.8 0.1 tile.21
  12.9 0.1 add.154
  12.9 0.1 tile.9
  13.0 0.0 copy-start.10
  13.1 0.6 copy-done.10
  13.7 0.2 fusion.46
  13.9 0.0 copy-done.2
  13.9 0.0 copy-done.6
  13.9 0.0 copy-start.8
  13.9 0.3 convolution_bitcast_fusion.5
  14.2 0.6 copy-done.8
  14.8 0.0 collective-permute-done
  14.9 0.4 collective-permute-done.1
  15.3 0.1 reshape_reshape_squeeze.10
  15.4 0.3 fusion.64
  15.7 0.2 fusion.4
  15.9 0.1 reshape_reshape_squeeze.9
  16.0 0.0 copy-start.1
  16.0 0.3 multiply_reduce_fusion.3
  16.4 0.7 copy-done.1
  17.0 0.0 copy-start
  17.0 0.2 convolution_bitcast_fusion.7
  17.3 0.8 copy-done
  18.1 0.2 convolution_bitcast_fusion.6
  18.3 1.3 convolution_bitcast_fusion.2
  19.7 1.4 convolution_bitcast_fusion.1
  21.1 1.3 convolution_bitcast_fusion
  22.4 0.0 all-reduce.3.cloned.1.call-update
  22.4 13.0 %psum.29 = f32[]{:T(128)} all-reduce(f32[]{:T(128)S(6)} %convert_element_type.263), channel_id=1, replica_groups=mesh['head'=2,'view'=4,'row'=4] {'view'}, use_global_device_ids=true, to_apply=%region_4.5 | all-reduce | flops 1 | bytes 8 | tf_op jit(solution)/shard_map/psum | solution.py:95
  35.5 95.8 %all-reduce.3.cloned.1.call-done = (f32[1,512,512]{2,1,0:T(8,128)}, f32[1,512,512]{2,1,0:T(8,128)}, f32[1,512,512]{2,1,0:T(8,128)}) async-done(((f32[1,512,512]{2,1,0:T(8,128)}, f32[1,512,512]{2,1,0:T(8,128)}, f32[1,512,512]{2,1,0:T(8,128)}), (f32[1,512,512]{2,1,0:T(8,128)}, f32[1,512,512]{2,1,0:T(8,128)}, f32[1,512,512]{2,1,0:T(8,128)})) %all-reduce.3.cloned.1.call-update) | async-done | bytes 3145744 | tf_op jit(solution)/shard_map/psum | solution.py:140
  131.2 0.0 copy-start.4
  131.3 2.2 %fusion.11 = (f32[512]{0:T(512)S(1)}, f32[512]{0:T(512)S(1)}) fusion(bf16[1,512,512]{2,1,0:T(8,128)(2,1)S(1)} %copy-done, f32[1,512,512]{2,1,0:T(8,128)} %get-tuple-element.11, f32[]{:T(128)} %psum.29), kind=kLoop, calls=%fused_computation.28 | loop fusion | flops 1833984 | bytes 1576964 | tf_op jit(solution)/shard_map/reduce_sum | solution.py:68
  133.5 0.0 copy-done.4
  133.5 0.0 copy-start.5
  133.5 2.5 %fusion.9 = (f32[512]{0:T(512)S(1)}, f32[512]{0:T(512)S(1)}, f32[512]{0:T(512)S(1)}, f32[512]{0:T(512)S(1)}) fusion(bf16[1,512,512]{2,1,0:T(8,128)(2,1)S(1)} %copy-done.2, f32[1,512,512]{2,1,0:T(8,128)S(1)} %copy-done.4, f32[]{:T(128)} %psum.29, f32[1,512,512]{2,1,0:T(8,128)} %get-tuple-element.13, bf16[1,512,512]{2,1,0:T(8,128)(2,1)S(1)} %copy-done.1), kind=kLoop, calls=%fused_computation.26 | loop fusion | flops 3667968 | bytes 3153924 | tf_op jit(solution)/shard_map/reduce_sum | solution.py:68
  136.0 0.0 copy-done.5
  136.0 0.0 copy-start.3
  136.0 1.0 convolution_bitcast_fusion.4
  137.0 0.2 copy-done.3
  137.2 3.0 %convolution_convert_fusion = bf16[512,128]{0,1:T(8,128)(2,1)} fusion(bf16[128,512]{0,1:T(8,128)(2,1)S(1)} %fusion.36, f32[512]{0:T(512)S(1)} %rsqrt_multiply_fusion, f32[512]{0:T(512)S(1)} %rsqrt_multiply_fusion.2, f32[128,1,512]{2,0,1:T(8,128)S(1)} %convolution_bitcast_fusion.4, bf16[1,512,512]{2,1,0:T(8,128)(2,1)S(1)} %copy-done.2, ...), kind=kOutput, calls=%fused_computation.22 | convolution fusion | flops 137297920 | bytes 3674116 | tf_op jit(solution)/shard_map/thj,hjo->tho/dot_general | solution.py:152
  (16 shorter events, 0.2 us)
Async XLA Ops:
  6.5 1.0 copy-start.7
  6.5 7.3 %copy-start.2 = (bf16[1,512,512]{2,1,0:T(8,128)(2,1)S(1)}, bf16[1,512,512]{2,1,0:T(8,128)(2,1)}, u32[]{:S(2)}) copy-start(bf16[1,512,512]{2,1,0:T(8,128)(2,1)} %param.19) | copy-start | bytes 1572868
  6.5 124.7 %all-reduce.3.cloned.1.call-start = ((), (), s32[]{:S(2)}) async-start(), calls=%async_computation | async-start | bytes 6291456 | tf_op jit(solution)/shard_map/psum | solution.py:140
  7.6 6.3 %copy-start.6 = (bf16[1,8,16,512]{3,2,1,0:T(8,128)(2,1)S(1)}, bf16[1,8,16,512]{3,2,1,0:T(8,128)(2,1)}, u32[]{:S(2)}) copy-start(bf16[1,8,16,512]{3,2,1,0:T(8,128)(2,1)} %param.13) | copy-start | bytes 393220
  7.6 7.3 %collective-permute-start = (bf16[2,2,16,512]{3,2,1,0:T(8,128)(2,1)S(1)}, bf16[2,2,16,512]{3,2,1,0:T(8,128)(2,1)S(1)}, u32[]{:S(2)}, u32[]{:S(2)}) collective-permute-start(bf16[2,2,16,512]{3,2,1,0:T(8,128)(2,1)S(1)} %get-tuple-element.20), channel_id=1, source_target_pairs={{0,1},{1,2},{2,3},{4,5},{5,6},{6,7},{8,9},{9,10},{10,11},{12,13},{... | collective-permute-start | bytes 196616 | tf_op jit(solution)/shard_map/ppermute | solution.py:20
  10.0 5.2 %collective-permute-start.1 = (bf16[2,2,16,512]{3,2,1,0:T(8,128)(2,1)S(1)}, bf16[2,2,16,512]{3,2,1,0:T(8,128)(2,1)S(1)}, u32[]{:S(2)}, u32[]{:S(2)}) collective-permute-start(bf16[2,2,16,512]{3,2,1,0:T(8,128)(2,1)S(1)} %get-tuple-element.21), channel_id=1, source_target_pairs={{1,0},{2,1},{3,2},{5,4},{6,5},{7,6},{9,8},{10,9},{11,10},{13,12},{... | collective-permute-start | bytes 196616 | tf_op jit(solution)/shard_map/ppermute | solution.py:21
  12.0 0.7 copy-start.9
  13.0 0.7 copy-start.10
  13.9 0.9 copy-start.8
  16.0 1.0 copy-start.1
  17.0 1.0 copy-start
  131.2 2.2 %copy-start.4 = (f32[1,512,512]{2,1,0:T(8,128)S(1)}, f32[1,512,512]{2,1,0:T(8,128)}, u32[]{:S(2)}) copy-start(f32[1,512,512]{2,1,0:T(8,128)} %get-tuple-element.12) | copy-start | bytes 3145732
  133.5 2.5 %copy-start.5 = (f32[1,512,512]{2,1,0:T(8,128)S(1)}, f32[1,512,512]{2,1,0:T(8,128)}, u32[]{:S(2)}) copy-start(f32[1,512,512]{2,1,0:T(8,128)} %get-tuple-element.13) | copy-start | bytes 3145732
  136.0 1.2 copy-start.3
Sparse Core Ops, SparseCore 0:
  22.5 108.6 all-reduce.2
where the time goes:
time: 148 us; the launch traced here: 147 us
  waiting for transfers between devices  96.2 us (65%)
  between operations  14.3 us (10%)
  blocking collectives  13 us (9%)
  matrix products  9.77 us (7%)
  local copies, waits for them, and re-layouts  5.1 us (3%)
  other arithmetic  4.98 us (3%)
  starting transfers between devices  3.69 us (2%)
    psum x1, waiting for transfers between devices, per_device(): lax.psum((grad_first, grad_third, grad_second), ('view', 'row'))  95.8 us
    psum x1, blocking collectives, per_device(): total_valid = lax.psum(view_total.astype(jnp.float32), 'view')  13 us
    reduce_sum x2, other arithmetic, renorm(): jnp.sum(old_rows * old_rows, -1, keepdims=True) + 1e-06  4.67 us
    unnamed x23, local copies, waits for them, and re-layouts  4.43 us
    dot_general x1, matrix products, per_device(): jnp.einsum('thj,hjo->tho', applied, new_second, preferred_element_type=jn...  3.03 us
  transfers between devices with their start and end apart: 3, of which 2 were waited for; matrix products, arithmetic and copies ran while one was open for 1% of the time, Pallas kernels for 0%

commit v1 on v0

--- a/solution.py
+++ b/solution.py
@@ -1,13 +1,21 @@
+import functools
 import math
 
 import jax
 import jax.numpy as jnp
 from jax import lax
+from jax.experimental import pallas as pl
+from jax.experimental.pallas import tpu as pltpu
 from jax.sharding import PartitionSpec as P
 
 HD = 512
 ATT_HD = 128
 HALO = 2
+MESH = pl.DeviceIdType.MESH
+BF16 = jnp.bfloat16
+F32 = jnp.float32
+NT = (((1,), (1,)), ((), ()))
+TN = (((0,), (0,)), ((), ()))
 
 
 def with_halo(value, sides, width):
@@ -155,6 +163,292 @@
     return fast_out.reshape(1, row_count, col_count, feat_width)
 
 
+def halve(values_in, size):
+    if size & (size - 1) == 0:
+        return values_in >> (size.bit_length() - 1)
+    return lax.div(values_in, jnp.int32(size))
+
+
+def dot(left, right, dims=(((1,), (0,)), ((), ()))):
+    return lax.dot_general(left, right, dims, preferred_element_type=F32)
+
+
+def lane_square_sums(matrix):
+    wide = matrix.astype(F32)
+    square = wide * wide
+    high = square.astype(BF16)
+    low = (square - high.astype(F32)).astype(BF16)
+    ones = jnp.ones((8, matrix.shape[1]), BF16)
+    return dot(ones, high, NT) + dot(ones, low, NT)
+
+
+def step_kernel(
+    nr, nz, cols,
+    q_ref, k_ref, v_ref, t_ref, rates_ref, reach_ref, count_ref, wf_hbm, wt_hbm, ws_hbm,
+    out_ref,
+    wf, wt, ws, halo, kall, sall, fac, fac_send, cnt, gfull, gsend, grecv,
+    wtr, news, ss, ssz, osend, orecv, load_sem, send_sem, recv_sem,
+):
+    tokens, width = q_ref.shape
+    rows_here = tokens // cols
+    hid = width // nr
+    part = hid // nz
+    edge = HALO * cols
+    me = lax.axis_index("row")
+    mz = lax.axis_index("view")
+
+    loads = [
+        pltpu.make_async_copy(source, target, load_sem.at[i])
+        for i, (source, target) in enumerate(((wf_hbm, wf), (wt_hbm, wt), (ws_hbm, ws)))
+    ]
+    for load in loads:
+        load.start()
+
+    def row_peer(shift):
+        return lax.rem(me + (shift + nr), nr)
+
+    def view_peer(shift):
+        return lax.rem(mz + (shift + nz), nz)
+
+    used = [0]
+
+    def send(source, target, axis, peer):
+        slot = used[0]
+        used[0] += 1
+        copy = pltpu.make_async_remote_copy(
+            src_ref=source, dst_ref=target,
+            send_sem=send_sem.at[slot], recv_sem=recv_sem.at[slot],
+            device_id={axis: peer}, device_id_type=MESH,
+        )
+        copy.start()
+        return copy
+
+    barrier = pltpu.get_barrier_semaphore()
+    for d in range(1, nr):
+        pl.semaphore_signal(barrier, inc=1, device_id={"row": row_peer(d)}, device_id_type=MESH)
+    for d in range(1, nz):
+        pl.semaphore_signal(barrier, inc=1, device_id={"view": view_peer(d)}, device_id_type=MESH)
+
+    row_base = me * rows_here
+    tok_base = me * tokens
+    view_total = count_ref[0]
+    sub = lax.broadcasted_iota(jnp.int32, (tokens, tokens), 0)
+    lane = lax.broadcasted_iota(jnp.int32, (tokens, tokens), 1)
+    rate_col = jnp.sum(jnp.where(sub == lane, rates_ref[...], 0.0), axis=1, keepdims=True)
+    tok_col = tok_base + lax.broadcasted_iota(jnp.int32, (tokens, 1), 0)
+    valid_col = (tok_col < view_total).astype(F32)
+    sall[0] = (rate_col * valid_col * t_ref[...].astype(F32)).astype(BF16)
+    cnt[0] = jnp.full((8, 128), view_total, jnp.int32).astype(F32)
+
+    pl.semaphore_wait(barrier, (nr - 1) + (nz - 1))
+
+    halo_copies = []
+    for i, ref in enumerate((k_ref, v_ref)):
+        halo_copies.append(send(ref.at[pl.ds(tokens - edge, edge)], halo.at[0, i], "row", row_peer(1)))
+        halo_copies.append(send(ref.at[pl.ds(0, edge)], halo.at[1, i], "row", row_peer(-1)))
+    s_copies = [send(sall.at[0], sall.at[d], "row", row_peer(d)) for d in range(1, nr)]
+    c_copies = [send(cnt.at[0], cnt.at[d], "view", view_peer(d)) for d in range(1, nz)]
+
+    span = tokens + 2 * edge
+    qi = lax.broadcasted_iota(jnp.int32, (tokens, span), 0)
+    ki = lax.broadcasted_iota(jnp.int32, (tokens, span), 1)
+    q_row = halve(qi, cols)
+    k_row = halve(ki, cols) - HALO
+    reach = jnp.zeros((tokens, span), jnp.int32)
+    for r in range(rows_here):
+        reach = jnp.where(q_row == r, reach_ref[r], reach)
+    k_abs = k_row + row_base
+    k_tok = ki - edge
+    allowed = (
+        (jnp.abs(k_row - q_row) <= reach)
+        & (k_abs >= 0)
+        & (k_abs < nr * rows_here)
+        & ((k_tok + tok_base < view_total) | (k_tok == qi))
+    )
+    for copy in halo_copies:
+        copy.wait()
+    pieces = []
+    total_sq = jnp.zeros((tokens, 1), F32)
+    for h in range(width // ATT_HD):
+        hs = slice(h * ATT_HD, (h + 1) * ATT_HD)
+        keys = jnp.concatenate([halo[0, 0, :, hs], k_ref[:, hs], halo[1, 0, :, hs]], axis=0)
+        vals = jnp.concatenate([halo[0, 1, :, hs], v_ref[:, hs], halo[1, 1, :, hs]], axis=0)
+        scores = dot(q_ref[:, hs], keys, NT) * (1.0 / math.sqrt(ATT_HD))
+        scores = jnp.where(allowed, scores, -1e30)
+        powers = jnp.exp(scores - jnp.max(scores, axis=-1, keepdims=True))
+        weights = (powers * (1.0 / jnp.sum(powers, axis=-1, keepdims=True))).astype(BF16)
+        piece = dot(weights, vals).astype(BF16).astype(F32)
+        total_sq = total_sq + jnp.sum(piece * piece, axis=-1, keepdims=True)
+        pieces.append(piece)
+    norm = lax.rsqrt(total_sq * (1.0 / width) + 1e-06)
+    for h, piece in enumerate(pieces):
+        kall[0, :, h * ATT_HD:(h + 1) * ATT_HD] = (piece * norm).astype(BF16)
+    k_copies = [send(kall.at[0], kall.at[d], "row", row_peer(d)) for d in range(1, nr)]
+
+    for load in loads:
+        load.wait()
+    f_copies = []
+    for d in list(range(1, nr)) + [0]:
+        mine = pl.ds(pl.multiple_of(row_peer(d) * hid, hid), hid)
+        first = dot(kall[0], wf[:, mine])
+        third = dot(kall[0], wt[:, mine])
+        back = dot(sall[0], ws[mine, :], NT)
+        sig = jax.nn.sigmoid(first)
+        gate = first * sig
+        parts = (
+            (back * third * (sig * (1.0 + first * (1.0 - sig)))).astype(BF16),
+            (back * gate).astype(BF16),
+            (gate * third).astype(BF16),
+        )
+        for m in range(3):
+            if d:
+                fac_send[d - 1, m] = parts[m]
+            else:
+                fac[0, m] = parts[m]
+        if d:
+            f_copies.append(send(fac_send.at[d - 1], fac.at[d], "row", row_peer(d)))
+
+    mine = pl.ds(pl.multiple_of(me * hid, hid), hid)
+    wtr[0] = wf[:, mine].astype(F32).T
+    wtr[1] = wt[:, mine].astype(F32).T
+    wtr[2] = ws[mine, :].astype(F32)
+    old_sums = [lane_square_sums(wf[...]), lane_square_sums(wt[...])]
+
+    for copy in s_copies + k_copies + f_copies:
+        copy.wait()
+
+    g_copies = []
+    for m in (2, 0, 1):
+        right = sall if m == 2 else kall
+        grad = dot(fac[0, m], right[0], TN)
+        for d in range(1, nr):
+            grad = grad + dot(fac[d, m], right[d], TN)
+        gfull[m] = grad
+        for z in range(nz):
+            gsend[z, m] = grad[z * part:(z + 1) * part].astype(BF16)
+        for d in range(1, nz):
+            g_copies.append(
+                send(gsend.at[view_peer(d), m], grecv.at[d - 1, m], "view", view_peer(d))
+            )
+    for copy in c_copies:
+        copy.wait()
+    total_valid = cnt[0, 0:1, 0:1]
+    for d in range(1, nz):
+        total_valid = total_valid + cnt[d, 0:1, 0:1]
+
+    here = pl.ds(pl.multiple_of(mz * part, part), part)
+    w_copies = []
+    sums = []
+    for i, m in enumerate((2, 0, 1)):
+        for copy in g_copies[i * (nz - 1):(i + 1) * (nz - 1)]:
+            copy.wait()
+        grad = gfull[m, here, :]
+        for d in range(1, nz):
+            grad = grad + grecv[d - 1, m].astype(F32)
+        old = wtr[m, here, :]
+        raised = old + grad / total_valid
+        if m == 2:
+            rescale = jnp.sqrt(jnp.sum(old * old, -1, keepdims=True) + 1e-06) / jnp.sqrt(
+                jnp.sum(raised * raised, -1, keepdims=True) + 1e-06
+            )
+            raised = raised * rescale
+        else:
+            sums.append(jnp.sum(raised * raised, axis=0, keepdims=True))
+        news[0, m] = raised.astype(BF16)
+        for d in range(1, nz):
+            w_copies.append(send(news.at[0, m], news.at[d, m], "view", view_peer(d)))
+    ss[0, 0:1] = sums[0]
+    ss[0, 1:2] = sums[1]
+    ss_copies = [send(ss.at[0], ss.at[d], "row", row_peer(d)) for d in range(1, nr)]
+    for copy in ss_copies:
+        copy.wait()
+    strip_sums = ss[0, 0:2]
+    for d in range(1, nr):
+        strip_sums = strip_sums + ss[d, 0:2]
+    ssz[0, 0:2] = strip_sums
+    ssz_copies = [send(ssz.at[0], ssz.at[d], "view", view_peer(d)) for d in range(1, nz)]
+    for copy in ssz_copies:
+        copy.wait()
+    new_sums = ssz[0, 0:2]
+    for d in range(1, nz):
+        new_sums = new_sums + ssz[d, 0:2]
+    scale_first = jnp.sqrt(old_sums[0][0:1] + 1e-06) / jnp.sqrt(new_sums[0:1] + 1e-06)
+    scale_third = jnp.sqrt(old_sums[1][0:1] + 1e-06) / jnp.sqrt(new_sums[1:2] + 1e-06)
+
+    for copy in w_copies:
+        copy.wait()
+    new_first, new_third, new_second = (
+        jnp.concatenate([news[d, m] for d in range(nz)], axis=0) for m in range(3)
+    )
+    o_copies = []
+    for d in list(range(1, nr)) + [0]:
+        keys = kall[d].astype(F32)
+        first = dot((keys * scale_first).astype(BF16), new_first, NT)
+        third = dot((keys * scale_third).astype(BF16), new_third, NT)
+        applied = (first * jax.nn.sigmoid(first) * third).astype(BF16)
+        share = dot(applied, new_second)
+        if d:
+            osend[d - 1] = share.astype(BF16)
+            o_copies.append(send(osend.at[d - 1], orecv.at[d - 1], "row", row_peer(-d)))
+    for copy in o_copies:
+        copy.wait()
+    for d in range(1, nr):
+        share = share + orecv[d - 1].astype(F32)
+    out_ref[...] = share.astype(BF16)
+
+
+def fused_step(
+    nr, nz,
+    query_feats, key_feats, value_feats, target, token_rates, row_reach, view_counts,
+    w_first, w_third, w_second,
+):
+    _, row_count, cols, width = query_feats.shape
+    tokens = row_count * cols
+    hid = width // nr
+    part = hid // nz
+    edge = HALO * cols
+    copies = 4 + 3 * (nr - 1) + (nz - 1) + 3 * (nz - 1) + 3 * (nz - 1) + (nr - 1) + (nz - 1) + (nr - 1)
+    vmem = pl.BlockSpec(memory_space=pltpu.VMEM)
+    smem = pl.BlockSpec(memory_space=pltpu.SMEM)
+    anywhere = pl.BlockSpec(memory_space=pl.ANY)
+    flat = lambda a: a.reshape(tokens, width)
+    out = pl.pallas_call(
+        functools.partial(step_kernel, nr, nz, cols),
+        out_shape=jax.ShapeDtypeStruct((tokens, width), BF16),
+        in_specs=[vmem] * 5 + [smem] * 2 + [anywhere] * 3,
+        out_specs=vmem,
+        scratch_shapes=[
+            pltpu.VMEM((width, width), BF16),
+            pltpu.VMEM((width, width), BF16),
+            pltpu.VMEM((width, width), BF16),
+            pltpu.VMEM((2, 2, edge, width), BF16),
+            pltpu.VMEM((nr, tokens, width), BF16),
+            pltpu.VMEM((nr, tokens, width), BF16),
+            pltpu.VMEM((nr, 3, tokens, hid), BF16),
+            pltpu.VMEM((nr - 1, 3, tokens, hid), BF16),
+            pltpu.VMEM((nz, 8, 128), F32),
+            pltpu.VMEM((3, hid, width), F32),
+            pltpu.VMEM((nz, 3, part, width), BF16),
+            pltpu.VMEM((nz - 1, 3, part, width), BF16),
+            pltpu.VMEM((3, hid, width), F32),
+            pltpu.VMEM((nz, 3, part, width), BF16),
+            pltpu.VMEM((nr, 8, width), F32),
+            pltpu.VMEM((nz, 8, width), F32),
+            pltpu.VMEM((nr - 1, tokens, width), BF16),
+            pltpu.VMEM((nr - 1, tokens, width), BF16),
+            pltpu.SemaphoreType.DMA((3,)),
+            pltpu.SemaphoreType.DMA((copies,)),
+            pltpu.SemaphoreType.DMA((copies,)),
+        ],
+        compiler_params=pltpu.CompilerParams(collective_id=0, has_side_effects=True),
+    )(
+        flat(query_feats), flat(key_feats), flat(value_feats), flat(target),
+        token_rates.reshape(1, tokens), row_reach, view_counts,
+        w_first.reshape(width, width), w_third.reshape(width, width), w_second.reshape(width, width),
+    )
+    return out.reshape(query_feats.shape)
+
+
 def solution(mesh):
     placed = (
         P("view", "row", None, "head"),
@@ -168,8 +462,10 @@
         P("head", None, None),
         P("head", None, None),
     )
+    nr, nz = mesh.shape["row"], mesh.shape["view"]
+    fits = nr > 1 and nz > 1 and HD % (128 * nr) == 0 and HD % (16 * nr * nz) == 0
     return jax.shard_map(
-        per_device,
+        functools.partial(fused_step, nr, nz) if fits else per_device,
         mesh=mesh,
         in_specs=placed,
         out_specs=P("view", "row", None, "head"),

time: 148 us -> 56.2 us (0.38)
  waiting for transfers between devices: 96.2 us -> 0 us
  Pallas kernels: 0 us -> 53.8 us
  between operations: 14.3 us -> 0.66 us
  blocking collectives: 13 us -> 0 us
  matrix products: 9.77 us -> 0 us
  other arithmetic: 4.98 us -> 0 us
  starting transfers between devices: 3.69 us -> 0 us
  local copies, waits for them, and re-layouts: 5.1 us -> 1.57 us
    psum x1 -> x0, waiting for transfers between devices: 95.8 us -> none  [per_device(): lax.psum((grad_first, grad_third, grad_second), ('view', 'row'))]
    pallas_call x0 -> x1, Pallas kernels: none -> 53.8 us  [fused_step(): pl.pallas_call(functools.partial(step_kernel, nr, nz, cols), out_shape=ja...]
    psum x1 -> x0, blocking collectives: 13 us -> none  [per_device(): total_valid = lax.psum(view_total.astype(jnp.float32), 'view')]
    dot_general x10 -> x0, matrix products: 9.47 us -> none  [the longest x1 3.03 us: per_device(): jnp.einsum('thj,hjo->tho', applied, new_second, preferred_element_type=jn...]
    reduce_sum x2 -> x0, other arithmetic: 4.67 us -> none  [renorm(): jnp.sum(old_rows * old_rows, -1, keepdims=True) + 1e-06]
    ppermute x2 -> x0, starting transfers between devices: 3.69 us -> none  [the longest x1 2.4 us: with_halo(): before = lax.ppermute(last, axis, up)]
    unnamed x23 -> x1, local copies, waits for them, and re-layouts: 4.43 us -> 1.57 us
  transfers between devices with their start and end apart: 3 -> 0, of which waited for: 2 -> 0; matrix products, arithmetic and copies ran while one was open for 1% -> 0% of each run, Pallas kernels for 0% -> 0%
where the time goes in v1:
time: 56.2 us; the launch traced here: 56 us
  Pallas kernels  53.8 us (96%)
  local copies, waits for them, and re-layouts  1.57 us (3%)
  between operations  0.66 us (1%)
    pallas_call x1, Pallas kernels, fused_step(): pl.pallas_call(functools.partial(step_kernel, nr, nz, cols), out_shape=ja...  53.8 us
    unnamed x1, local copies, waits for them, and re-layouts  1.57 us

profile of v1, /device:TPU:0, one launch (start us, length us, event | category | flops | bytes accessed | tf_op | source)
XLA Modules:
  0.0 56.0 jit_solution(13707247403995188184)
XLA Ops:
  0.7 53.8 %shard_map.100 = bf16[128,512]{1,0:T(8,128)(2,1)} custom-call(bf16[128,512]{1,0:T(8,128)(2,1)} %bitcast.13, bf16[128,512]{1,0:T(8,128)(2,1)} %bitcast.14, bf16[128,512]{1,0:T(8,128)(2,1)} %bitcast.15, bf16[128,512]{1,0:T(8,128)(2,1)} %bitcast.16, f32[1,128]{1,0:T(1,128)} %bitcast.17, s32[8]{0:T(128)} %reach_ref.1, s32[1]{0:T(128)S(6)} %copy.12.count_ref, ...), custom_call_target="tpu_custom_call" | custom-call | tf_op jit(solution)/shard_map/pallas_call | solution.py:415
  54.4 1.6 %copy.13 = bf16[1,8,16,512]{3,2,1,0:T(8,128)(2,1)} copy(bf16[1,8,16,512]{3,2,1,0:T(8,128)(2,1)} %bitcast.12) | data formatting | bytes 262144

commit v2 on v1

--- a/solution.py
+++ b/solution.py
@@ -173,20 +173,20 @@
     return lax.dot_general(left, right, dims, preferred_element_type=F32)
 
 
-def lane_square_sums(matrix):
-    wide = matrix.astype(F32)
-    square = wide * wide
-    high = square.astype(BF16)
-    low = (square - high.astype(F32)).astype(BF16)
-    ones = jnp.ones((8, matrix.shape[1]), BF16)
-    return dot(ones, high, NT) + dot(ones, low, NT)
+def flip(index, bits):
+    bit = 1
+    while bit <= bits:
+        if bits & bit:
+            index = index + bit - 2 * bit * lax.rem(lax.div(index, bit), 2)
+        bit *= 2
+    return index
 
 
 def step_kernel(
     nr, nz, cols,
-    q_ref, k_ref, v_ref, t_ref, rates_ref, reach_ref, count_ref, wf_hbm, wt_hbm, ws_hbm,
+    q_hbm, k_hbm, v_hbm, t_hbm, rates_hbm, reach_ref, count_ref, wf_hbm, wt_hbm, ws_hbm,
     out_ref,
-    wf, wt, ws, halo, kall, sall, fac, fac_send, cnt, gfull, gsend, grecv,
+    q_ref, k_ref, v_ref, t_ref, rates_ref, wf, wt, ws, halo, kall, sall, cnt, gfull, gsend, grecv,
     wtr, news, ss, ssz, osend, orecv, load_sem, send_sem, recv_sem,
 ):
     tokens, width = q_ref.shape
@@ -194,18 +194,21 @@
     hid = width // nr
     part = hid // nz
     edge = HALO * cols
+    heads = width // ATT_HD
     me = lax.axis_index("row")
     mz = lax.axis_index("view")
+    mine = pl.ds(pl.multiple_of(me * hid, hid), hid)
+    here = pl.ds(pl.multiple_of(mz * part, part), part)
 
     loads = [
         pltpu.make_async_copy(source, target, load_sem.at[i])
-        for i, (source, target) in enumerate(((wf_hbm, wf), (wt_hbm, wt), (ws_hbm, ws)))
+        for i, (source, target) in enumerate((
+            (k_hbm, k_ref), (v_hbm, v_ref), (t_hbm, t_ref), (rates_hbm, rates_ref), (q_hbm, q_ref),
+            (wf_hbm.at[:, mine], wf), (wt_hbm.at[:, mine], wt), (ws_hbm.at[mine, :], ws),
+        ))
     ]
     for load in loads:
         load.start()
-
-    def row_peer(shift):
-        return lax.rem(me + (shift + nr), nr)
 
     def view_peer(shift):
         return lax.rem(mz + (shift + nz), nz)
@@ -223,124 +226,145 @@
         copy.start()
         return copy
 
+    def spread(ref):
+        return {d: send(ref.at[0], ref.at[d], "row", flip(me, d)) for d in [1] + list(range(2, nr, 2))}
+
+    def hand_on(ref, copies):
+        for d in range(2, nr, 2):
+            copies[d].wait_recv()
+            copies[d + 1] = send(ref.at[d], ref.at[d + 1], "row", flip(me, 1))
+
+    def settle(copies):
+        for d in copies:
+            copies[d].wait_send()
+
     barrier = pltpu.get_barrier_semaphore()
     for d in range(1, nr):
-        pl.semaphore_signal(barrier, inc=1, device_id={"row": row_peer(d)}, device_id_type=MESH)
+        pl.semaphore_signal(barrier, inc=1, device_id={"row": flip(me, d)}, device_id_type=MESH)
     for d in range(1, nz):
         pl.semaphore_signal(barrier, inc=1, device_id={"view": view_peer(d)}, device_id_type=MESH)
+    above = lax.rem(me + 1, nr)
+    below = lax.rem(me + (nr - 1), nr)
 
     row_base = me * rows_here
     tok_base = me * tokens
     view_total = count_ref[0]
+    cnt[0] = jnp.full((8, 128), view_total, jnp.int32).astype(F32)
     sub = lax.broadcasted_iota(jnp.int32, (tokens, tokens), 0)
     lane = lax.broadcasted_iota(jnp.int32, (tokens, tokens), 1)
-    rate_col = jnp.sum(jnp.where(sub == lane, rates_ref[...], 0.0), axis=1, keepdims=True)
     tok_col = tok_base + lax.broadcasted_iota(jnp.int32, (tokens, 1), 0)
     valid_col = (tok_col < view_total).astype(F32)
+    for load in loads[2:4]:
+        load.wait()
+    rate_col = jnp.sum(jnp.where(sub == lane, rates_ref[...], 0.0), axis=1, keepdims=True)
     sall[0] = (rate_col * valid_col * t_ref[...].astype(F32)).astype(BF16)
-    cnt[0] = jnp.full((8, 128), view_total, jnp.int32).astype(F32)
+    for load in loads[:2]:
+        load.wait()
 
     pl.semaphore_wait(barrier, (nr - 1) + (nz - 1))
 
     halo_copies = []
     for i, ref in enumerate((k_ref, v_ref)):
-        halo_copies.append(send(ref.at[pl.ds(tokens - edge, edge)], halo.at[0, i], "row", row_peer(1)))
-        halo_copies.append(send(ref.at[pl.ds(0, edge)], halo.at[1, i], "row", row_peer(-1)))
-    s_copies = [send(sall.at[0], sall.at[d], "row", row_peer(d)) for d in range(1, nr)]
+        halo_copies.append(send(ref.at[pl.ds(tokens - edge, edge)], halo.at[i, pl.ds(0, edge)], "row", above))
+        halo_copies.append(send(ref.at[pl.ds(0, edge)], halo.at[i, pl.ds(edge, edge)], "row", below))
+    s_copies = spread(sall)
     c_copies = [send(cnt.at[0], cnt.at[d], "view", view_peer(d)) for d in range(1, nz)]
 
-    span = tokens + 2 * edge
-    qi = lax.broadcasted_iota(jnp.int32, (tokens, span), 0)
-    ki = lax.broadcasted_iota(jnp.int32, (tokens, span), 1)
-    q_row = halve(qi, cols)
-    k_row = halve(ki, cols) - HALO
-    reach = jnp.zeros((tokens, span), jnp.int32)
-    for r in range(rows_here):
-        reach = jnp.where(q_row == r, reach_ref[r], reach)
-    k_abs = k_row + row_base
-    k_tok = ki - edge
-    allowed = (
-        (jnp.abs(k_row - q_row) <= reach)
-        & (k_abs >= 0)
-        & (k_abs < nr * rows_here)
-        & ((k_tok + tok_base < view_total) | (k_tok == qi))
-    )
+    def allowed(q_tok, k_tok):
+        q_row = halve(q_tok, cols)
+        k_row = halve(k_tok + edge, cols) - HALO
+        reach = jnp.zeros(q_tok.shape, jnp.int32)
+        for r in range(rows_here):
+            reach = jnp.where(q_row == r, reach_ref[r], reach)
+        k_abs = k_row + row_base
+        return (
+            (jnp.abs(k_row - q_row) <= reach)
+            & (k_abs >= 0)
+            & (k_abs < nr * rows_here)
+            & ((k_tok + tok_base < view_total) | (k_tok == q_tok))
+        )
+
+    near_ok = allowed(sub, lane)
+    far_q = lax.broadcasted_iota(jnp.int32, (tokens, 2 * edge), 0)
+    far_k = lax.broadcasted_iota(jnp.int32, (tokens, 2 * edge), 1)
+    far_ok = allowed(far_q, jnp.where(far_k < edge, far_k - edge, far_k - edge + tokens))
+    root = 1.0 / math.sqrt(ATT_HD)
+    spans = [slice(h * ATT_HD, (h + 1) * ATT_HD) for h in range(heads)]
+    loads[4].wait()
+    near = [
+        jnp.where(near_ok, dot(q_ref[:, hs], k_ref[:, hs], NT) * root, -1e30) for hs in spans
+    ]
+    near_top = [jnp.max(scores, axis=-1, keepdims=True) for scores in near]
+    for load in loads[5:]:
+        load.wait()
+    wtr[0] = wf[...].astype(F32).T
+    wtr[1] = wt[...].astype(F32).T
+    wtr[2] = ws[...].astype(F32)
     for copy in halo_copies:
         copy.wait()
     pieces = []
     total_sq = jnp.zeros((tokens, 1), F32)
-    for h in range(width // ATT_HD):
-        hs = slice(h * ATT_HD, (h + 1) * ATT_HD)
-        keys = jnp.concatenate([halo[0, 0, :, hs], k_ref[:, hs], halo[1, 0, :, hs]], axis=0)
-        vals = jnp.concatenate([halo[0, 1, :, hs], v_ref[:, hs], halo[1, 1, :, hs]], axis=0)
-        scores = dot(q_ref[:, hs], keys, NT) * (1.0 / math.sqrt(ATT_HD))
-        scores = jnp.where(allowed, scores, -1e30)
-        powers = jnp.exp(scores - jnp.max(scores, axis=-1, keepdims=True))
-        weights = (powers * (1.0 / jnp.sum(powers, axis=-1, keepdims=True))).astype(BF16)
-        piece = dot(weights, vals).astype(BF16).astype(F32)
+    for h, hs in enumerate(spans):
+        far = jnp.where(far_ok, dot(q_ref[:, hs], halo[0, :, hs], NT) * root, -1e30)
+        top = jnp.maximum(near_top[h], jnp.max(far, axis=-1, keepdims=True))
+        near_pow = jnp.exp(near[h] - top)
+        far_pow = jnp.exp(far - top)
+        inverse = 1.0 / (
+            jnp.sum(near_pow, axis=-1, keepdims=True) + jnp.sum(far_pow, axis=-1, keepdims=True)
+        )
+        piece = dot((near_pow * inverse).astype(BF16), v_ref[:, hs]) + dot(
+            (far_pow * inverse).astype(BF16), halo[1, :, hs]
+        )
+        piece = piece.astype(BF16).astype(F32)
         total_sq = total_sq + jnp.sum(piece * piece, axis=-1, keepdims=True)
         pieces.append(piece)
     norm = lax.rsqrt(total_sq * (1.0 / width) + 1e-06)
-    for h, piece in enumerate(pieces):
-        kall[0, :, h * ATT_HD:(h + 1) * ATT_HD] = (piece * norm).astype(BF16)
-    k_copies = [send(kall.at[0], kall.at[d], "row", row_peer(d)) for d in range(1, nr)]
-
-    for load in loads:
-        load.wait()
-    f_copies = []
-    for d in list(range(1, nr)) + [0]:
-        mine = pl.ds(pl.multiple_of(row_peer(d) * hid, hid), hid)
-        first = dot(kall[0], wf[:, mine])
-        third = dot(kall[0], wt[:, mine])
-        back = dot(sall[0], ws[mine, :], NT)
+    for hs, piece in zip(spans, pieces):
+        kall[0, :, hs] = (piece * norm).astype(BF16)
+    k_copies = spread(kall)
+    hand_on(sall, s_copies)
+
+    def gradients(d):
+        first = dot(kall[d], wf[...])
+        third = dot(kall[d], wt[...])
+        back = dot(sall[d], ws[...], NT)
         sig = jax.nn.sigmoid(first)
         gate = first * sig
-        parts = (
-            (back * third * (sig * (1.0 + first * (1.0 - sig)))).astype(BF16),
-            (back * gate).astype(BF16),
-            (gate * third).astype(BF16),
-        )
-        for m in range(3):
-            if d:
-                fac_send[d - 1, m] = parts[m]
-            else:
-                fac[0, m] = parts[m]
-        if d:
-            f_copies.append(send(fac_send.at[d - 1], fac.at[d], "row", row_peer(d)))
-
-    mine = pl.ds(pl.multiple_of(me * hid, hid), hid)
-    wtr[0] = wf[:, mine].astype(F32).T
-    wtr[1] = wt[:, mine].astype(F32).T
-    wtr[2] = ws[mine, :].astype(F32)
-    old_sums = [lane_square_sums(wf[...]), lane_square_sums(wt[...])]
-
-    for copy in s_copies + k_copies + f_copies:
-        copy.wait()
-
+        return (
+            dot((back * third * (sig * (1.0 + first * (1.0 - sig)))).astype(BF16), kall[d], TN),
+            dot((back * gate).astype(BF16), kall[d], TN),
+            dot((gate * third).astype(BF16), sall[d], TN),
+        )
+
+    for m, grad in enumerate(gradients(0)):
+        gfull[m] = grad
+    for d in [1] + list(range(2, nr, 2)) + list(range(3, nr, 2)):
+        if d == 2:
+            hand_on(kall, k_copies)
+        if d % 2:
+            k_copies[d].wait_recv()
+            s_copies[d].wait_recv()
+        for m, grad in enumerate(gradients(d)):
+            gfull[m] += grad
     g_copies = []
-    for m in (2, 0, 1):
-        right = sall if m == 2 else kall
-        grad = dot(fac[0, m], right[0], TN)
-        for d in range(1, nr):
-            grad = grad + dot(fac[d, m], right[d], TN)
-        gfull[m] = grad
+    for m in range(3):
         for z in range(nz):
-            gsend[z, m] = grad[z * part:(z + 1) * part].astype(BF16)
+            gsend[z, m] = gfull[m, z * part:(z + 1) * part, :].astype(BF16)
         for d in range(1, nz):
             g_copies.append(
                 send(gsend.at[view_peer(d), m], grecv.at[d - 1, m], "view", view_peer(d))
             )
+    ss[0, 2:3] = jnp.sum(wtr[0] * wtr[0], axis=0, keepdims=True)
+    ss[0, 3:4] = jnp.sum(wtr[1] * wtr[1], axis=0, keepdims=True)
     for copy in c_copies:
         copy.wait()
     total_valid = cnt[0, 0:1, 0:1]
     for d in range(1, nz):
         total_valid = total_valid + cnt[d, 0:1, 0:1]
 
-    here = pl.ds(pl.multiple_of(mz * part, part), part)
     w_copies = []
-    sums = []
-    for i, m in enumerate((2, 0, 1)):
-        for copy in g_copies[i * (nz - 1):(i + 1) * (nz - 1)]:
+    for m in range(3):
+        for copy in g_copies[m * (nz - 1):(m + 1) * (nz - 1)]:
             copy.wait()
         grad = gfull[m, here, :]
         for d in range(1, nz):
@@ -353,48 +377,56 @@
             )
             raised = raised * rescale
         else:
-            sums.append(jnp.sum(raised * raised, axis=0, keepdims=True))
+            ss[0, m:m + 1] = jnp.sum(raised * raised, axis=0, keepdims=True)
         news[0, m] = raised.astype(BF16)
         for d in range(1, nz):
             w_copies.append(send(news.at[0, m], news.at[d, m], "view", view_peer(d)))
-    ss[0, 0:1] = sums[0]
-    ss[0, 1:2] = sums[1]
-    ss_copies = [send(ss.at[0], ss.at[d], "row", row_peer(d)) for d in range(1, nr)]
+        if m == 1:
+            ss_copies = [send(ss.at[0], ss.at[d], "row", flip(me, d)) for d in range(1, nr)]
     for copy in ss_copies:
         copy.wait()
-    strip_sums = ss[0, 0:2]
+    strip_sums = ss[0]
     for d in range(1, nr):
-        strip_sums = strip_sums + ss[d, 0:2]
-    ssz[0, 0:2] = strip_sums
+        strip_sums = strip_sums + ss[d]
+    ssz[0] = strip_sums[0:2]
     ssz_copies = [send(ssz.at[0], ssz.at[d], "view", view_peer(d)) for d in range(1, nz)]
     for copy in ssz_copies:
         copy.wait()
-    new_sums = ssz[0, 0:2]
+    new_sums = ssz[0]
     for d in range(1, nz):
-        new_sums = new_sums + ssz[d, 0:2]
-    scale_first = jnp.sqrt(old_sums[0][0:1] + 1e-06) / jnp.sqrt(new_sums[0:1] + 1e-06)
-    scale_third = jnp.sqrt(old_sums[1][0:1] + 1e-06) / jnp.sqrt(new_sums[1:2] + 1e-06)
+        new_sums = new_sums + ssz[d]
+    scales = jnp.sqrt(strip_sums[2:4] + 1e-06) / jnp.sqrt(new_sums + 1e-06)
 
     for copy in w_copies:
         copy.wait()
     new_first, new_third, new_second = (
         jnp.concatenate([news[d, m] for d in range(nz)], axis=0) for m in range(3)
     )
-    o_copies = []
-    for d in list(range(1, nr)) + [0]:
+
+    def share(d):
         keys = kall[d].astype(F32)
-        first = dot((keys * scale_first).astype(BF16), new_first, NT)
-        third = dot((keys * scale_third).astype(BF16), new_third, NT)
-        applied = (first * jax.nn.sigmoid(first) * third).astype(BF16)
-        share = dot(applied, new_second)
-        if d:
-            osend[d - 1] = share.astype(BF16)
-            o_copies.append(send(osend.at[d - 1], orecv.at[d - 1], "row", row_peer(-d)))
-    for copy in o_copies:
-        copy.wait()
-    for d in range(1, nr):
-        share = share + orecv[d - 1].astype(F32)
-    out_ref[...] = share.astype(BF16)
+        first = dot((keys * scales[0:1]).astype(BF16), new_first, NT)
+        third = dot((keys * scales[1:2]).astype(BF16), new_third, NT)
+        return dot((first * jax.nn.sigmoid(first) * third).astype(BF16), new_second)
+
+    o_copies = {}
+    for d in list(range(3, nr, 2)) + list(range(2, nr, 2)) + [1, 0]:
+        total = share(d)
+        if d == 0:
+            continue
+        if d % 2 == 0:
+            o_copies[d + 1].wait_recv()
+            total = total + orecv[d].astype(F32)
+        osend[d - 1] = total.astype(BF16)
+        o_copies[d] = send(
+            osend.at[d - 1], orecv.at[d - 1], "row", flip(me, 1) if d % 2 else flip(me, d)
+        )
+    for d in [1] + list(range(2, nr, 2)):
+        o_copies[d].wait_recv()
+        total = total + orecv[d - 1].astype(F32)
+    out_ref[...] = total.astype(BF16)
+    for copies in (s_copies, k_copies, o_copies):
+        settle(copies)
 
 
 def fused_step(
@@ -407,36 +439,38 @@
     hid = width // nr
     part = hid // nz
     edge = HALO * cols
-    copies = 4 + 3 * (nr - 1) + (nz - 1) + 3 * (nz - 1) + 3 * (nz - 1) + (nr - 1) + (nz - 1) + (nr - 1)
-    vmem = pl.BlockSpec(memory_space=pltpu.VMEM)
+    copies = 4 + 4 * (nr - 1) + 8 * (nz - 1)
     smem = pl.BlockSpec(memory_space=pltpu.SMEM)
     anywhere = pl.BlockSpec(memory_space=pl.ANY)
     flat = lambda a: a.reshape(tokens, width)
     out = pl.pallas_call(
         functools.partial(step_kernel, nr, nz, cols),
         out_shape=jax.ShapeDtypeStruct((tokens, width), BF16),
-        in_specs=[vmem] * 5 + [smem] * 2 + [anywhere] * 3,
-        out_specs=vmem,
+        in_specs=[anywhere] * 5 + [smem] * 2 + [anywhere] * 3,
+        out_specs=pl.BlockSpec(memory_space=pltpu.VMEM),
         scratch_shapes=[
-            pltpu.VMEM((width, width), BF16),
-            pltpu.VMEM((width, width), BF16),
-            pltpu.VMEM((width, width), BF16),
-            pltpu.VMEM((2, 2, edge, width), BF16),
+            pltpu.VMEM((tokens, width), BF16),
+            pltpu.VMEM((tokens, width), BF16),
+            pltpu.VMEM((tokens, width), BF16),
+            pltpu.VMEM((tokens, width), BF16),
+            pltpu.VMEM((1, tokens), F32),
+            pltpu.VMEM((width, hid), BF16),
+            pltpu.VMEM((width, hid), BF16),
+            pltpu.VMEM((hid, width), BF16),
+            pltpu.VMEM((2, 2 * edge, width), BF16),
             pltpu.VMEM((nr, tokens, width), BF16),
             pltpu.VMEM((nr, tokens, width), BF16),
-            pltpu.VMEM((nr, 3, tokens, hid), BF16),
-            pltpu.VMEM((nr - 1, 3, tokens, hid), BF16),
             pltpu.VMEM((nz, 8, 128), F32),
             pltpu.VMEM((3, hid, width), F32),
             pltpu.VMEM((nz, 3, part, width), BF16),
             pltpu.VMEM((nz - 1, 3, part, width), BF16),
             pltpu.VMEM((3, hid, width), F32),
             pltpu.VMEM((nz, 3, part, width), BF16),
-            pltpu.VMEM((nr, 8, width), F32),
-            pltpu.VMEM((nz, 8, width), F32),
+            pltpu.VMEM((nr, 4, width), F32),
+            pltpu.VMEM((nz, 2, width), F32),
             pltpu.VMEM((nr - 1, tokens, width), BF16),
             pltpu.VMEM((nr - 1, tokens, width), BF16),
-            pltpu.SemaphoreType.DMA((3,)),
+            pltpu.SemaphoreType.DMA((8,)),
             pltpu.SemaphoreType.DMA((copies,)),
             pltpu.SemaphoreType.DMA((copies,)),
         ],
@@ -463,7 +497,8 @@
         P("head", None, None),
     )
     nr, nz = mesh.shape["row"], mesh.shape["view"]
-    fits = nr > 1 and nz > 1 and HD % (128 * nr) == 0 and HD % (16 * nr * nz) == 0
+    pairs = nr > 1 and nr & (nr - 1) == 0
+    fits = pairs and nz > 1 and HD % (128 * nr) == 0 and HD % (16 * nr * nz) == 0
     return jax.shard_map(
         functools.partial(fused_step, nr, nz) if fits else per_device,
         mesh=mesh,

time: 56.2 us -> 44.8 us (0.80)
  Pallas kernels: 53.8 us -> 42.4 us
    pallas_call x1, Pallas kernels: 53.8 us -> 42.4 us  [fused_step(): pl.pallas_call(functools.partial(step_kernel, nr, nz, cols), out_shape=ja...]
where the time goes in v2:
time: 44.8 us; the launch traced here: 44.6 us
  Pallas kernels  42.4 us (95%)
  local copies, waits for them, and re-layouts  1.57 us (4%)
  between operations  0.66 us (1%)
    pallas_call x1, Pallas kernels, fused_step(): pl.pallas_call(functools.partial(step_kernel, nr, nz, cols), out_shape=ja...  42.4 us
    unnamed x1, local copies, waits for them, and re-layouts  1.57 us

profile of v2, /device:TPU:0, one launch (start us, length us, event | category | flops | bytes accessed | tf_op | source)
XLA Modules:
  0.0 44.6 jit_solution(4520682774459357817)
XLA Ops:
  0.7 42.4 %shard_map.100 = bf16[128,512]{1,0:T(8,128)(2,1)} custom-call(bf16[128,512]{1,0:T(8,128)(2,1)} %bitcast.13, bf16[128,512]{1,0:T(8,128)(2,1)} %bitcast.14, bf16[128,512]{1,0:T(8,128)(2,1)} %bitcast.15, bf16[128,512]{1,0:T(8,128)(2,1)} %bitcast.16, f32[1,128]{1,0:T(1,128)} %bitcast.17, s32[8]{0:T(128)} %reach_ref.1, s32[1]{0:T(128)S(6)} %copy.12.count_ref, ...), custom_call_target="tpu_custom_call" | custom-call | tf_op jit(solution)/shard_map/pallas_call | solution.py:446
  43.0 1.6 %copy.13 = bf16[1,8,16,512]{3,2,1,0:T(8,128)(2,1)} copy(bf16[1,8,16,512]{3,2,1,0:T(8,128)(2,1)} %bitcast.12) | data formatting | bytes 262144

commit v3 on v2

--- a/solution.py
+++ b/solution.py
@@ -184,9 +184,9 @@
 
 def step_kernel(
     nr, nz, cols,
-    q_hbm, k_hbm, v_hbm, t_hbm, rates_hbm, reach_ref, count_ref, wf_hbm, wt_hbm, ws_hbm,
+    q_hbm, k_hbm, v_hbm, t_hbm, rates_hbm, reach_hbm, count_hbm, wf_hbm, wt_hbm, ws_hbm,
     out_ref,
-    q_ref, k_ref, v_ref, t_ref, rates_ref, wf, wt, ws, halo, kall, sall, cnt, gfull, gsend, grecv,
+    q_ref, k_ref, v_ref, t_ref, rates_ref, reach_ref, count_ref, wf, wt, ws, halo, raw, kall, sall, cnt, gfull, gsend, grecv,
     wtr, news, ss, ssz, osend, orecv, load_sem, send_sem, recv_sem,
 ):
     tokens, width = q_ref.shape
@@ -200,18 +200,24 @@
     mine = pl.ds(pl.multiple_of(me * hid, hid), hid)
     here = pl.ds(pl.multiple_of(mz * part, part), part)
 
+    def view_peer(shift):
+        return lax.rem(mz + (shift + nz), nz)
+
+    barrier = pltpu.get_barrier_semaphore()
+    for d in range(1, nr):
+        pl.semaphore_signal(barrier, inc=1, device_id={"row": flip(me, d)}, device_id_type=MESH)
+    for d in range(1, nz):
+        pl.semaphore_signal(barrier, inc=1, device_id={"view": view_peer(d)}, device_id_type=MESH)
     loads = [
         pltpu.make_async_copy(source, target, load_sem.at[i])
         for i, (source, target) in enumerate((
-            (k_hbm, k_ref), (v_hbm, v_ref), (t_hbm, t_ref), (rates_hbm, rates_ref), (q_hbm, q_ref),
+            (count_hbm, count_ref), (reach_hbm, reach_ref), (k_hbm, k_ref), (v_hbm, v_ref),
+            (t_hbm, t_ref), (rates_hbm, rates_ref), (q_hbm, q_ref),
             (wf_hbm.at[:, mine], wf), (wt_hbm.at[:, mine], wt), (ws_hbm.at[mine, :], ws),
         ))
     ]
     for load in loads:
         load.start()
-
-    def view_peer(shift):
-        return lax.rem(mz + (shift + nz), nz)
 
     used = [0]
 
@@ -226,49 +232,37 @@
         copy.start()
         return copy
 
-    def spread(ref):
-        return {d: send(ref.at[0], ref.at[d], "row", flip(me, d)) for d in [1] + list(range(2, nr, 2))}
-
-    def hand_on(ref, copies):
+    straight = [1] + list(range(2, nr, 2))
+
+    def spread(at):
+        return {d: send(at(0), at(d), "row", flip(me, d)) for d in straight}
+
+    def hand_on(at, copies):
         for d in range(2, nr, 2):
             copies[d].wait_recv()
-            copies[d + 1] = send(ref.at[d], ref.at[d + 1], "row", flip(me, 1))
+            copies[d + 1] = send(at(d), at(d + 1), "row", flip(me, 1))
 
     def settle(copies):
         for d in copies:
             copies[d].wait_send()
 
-    barrier = pltpu.get_barrier_semaphore()
-    for d in range(1, nr):
-        pl.semaphore_signal(barrier, inc=1, device_id={"row": flip(me, d)}, device_id_type=MESH)
-    for d in range(1, nz):
-        pl.semaphore_signal(barrier, inc=1, device_id={"view": view_peer(d)}, device_id_type=MESH)
     above = lax.rem(me + 1, nr)
     below = lax.rem(me + (nr - 1), nr)
 
     row_base = me * rows_here
     tok_base = me * tokens
+    for load in loads[:2]:
+        load.wait()
     view_total = count_ref[0]
     cnt[0] = jnp.full((8, 128), view_total, jnp.int32).astype(F32)
     sub = lax.broadcasted_iota(jnp.int32, (tokens, tokens), 0)
     lane = lax.broadcasted_iota(jnp.int32, (tokens, tokens), 1)
     tok_col = tok_base + lax.broadcasted_iota(jnp.int32, (tokens, 1), 0)
     valid_col = (tok_col < view_total).astype(F32)
-    for load in loads[2:4]:
+    for load in loads[2:6]:
         load.wait()
     rate_col = jnp.sum(jnp.where(sub == lane, rates_ref[...], 0.0), axis=1, keepdims=True)
     sall[0] = (rate_col * valid_col * t_ref[...].astype(F32)).astype(BF16)
-    for load in loads[:2]:
-        load.wait()
-
-    pl.semaphore_wait(barrier, (nr - 1) + (nz - 1))
-
-    halo_copies = []
-    for i, ref in enumerate((k_ref, v_ref)):
-        halo_copies.append(send(ref.at[pl.ds(tokens - edge, edge)], halo.at[i, pl.ds(0, edge)], "row", above))
-        halo_copies.append(send(ref.at[pl.ds(0, edge)], halo.at[i, pl.ds(edge, edge)], "row", below))
-    s_copies = spread(sall)
-    c_copies = [send(cnt.at[0], cnt.at[d], "view", view_peer(d)) for d in range(1, nz)]
 
     def allowed(q_tok, k_tok):
         q_row = halve(q_tok, cols)
@@ -290,20 +284,28 @@
     far_ok = allowed(far_q, jnp.where(far_k < edge, far_k - edge, far_k - edge + tokens))
     root = 1.0 / math.sqrt(ATT_HD)
     spans = [slice(h * ATT_HD, (h + 1) * ATT_HD) for h in range(heads)]
-    loads[4].wait()
+    loads[6].wait()
     near = [
         jnp.where(near_ok, dot(q_ref[:, hs], k_ref[:, hs], NT) * root, -1e30) for hs in spans
     ]
     near_top = [jnp.max(scores, axis=-1, keepdims=True) for scores in near]
-    for load in loads[5:]:
+
+    pl.semaphore_wait(barrier, (nr - 1) + (nz - 1))
+
+    halo_copies = []
+    for i, ref in enumerate((k_ref, v_ref)):
+        halo_copies.append(send(ref.at[pl.ds(tokens - edge, edge)], halo.at[i, pl.ds(0, edge)], "row", above))
+        halo_copies.append(send(ref.at[pl.ds(0, edge)], halo.at[i, pl.ds(edge, edge)], "row", below))
+    s_copies = spread(lambda d: sall.at[d])
+    c_copies = [send(cnt.at[0], cnt.at[d], "view", view_peer(d)) for d in range(1, nz)]
+    for load in loads[7:]:
         load.wait()
     wtr[0] = wf[...].astype(F32).T
     wtr[1] = wt[...].astype(F32).T
     wtr[2] = ws[...].astype(F32)
     for copy in halo_copies:
         copy.wait()
-    pieces = []
-    total_sq = jnp.zeros((tokens, 1), F32)
+    k_copies = []
     for h, hs in enumerate(spans):
         far = jnp.where(far_ok, dot(q_ref[:, hs], halo[0, :, hs], NT) * root, -1e30)
         top = jnp.maximum(near_top[h], jnp.max(far, axis=-1, keepdims=True))
@@ -315,45 +317,53 @@
         piece = dot((near_pow * inverse).astype(BF16), v_ref[:, hs]) + dot(
             (far_pow * inverse).astype(BF16), halo[1, :, hs]
         )
-        piece = piece.astype(BF16).astype(F32)
-        total_sq = total_sq + jnp.sum(piece * piece, axis=-1, keepdims=True)
-        pieces.append(piece)
-    norm = lax.rsqrt(total_sq * (1.0 / width) + 1e-06)
-    for hs, piece in zip(spans, pieces):
-        kall[0, :, hs] = (piece * norm).astype(BF16)
-    k_copies = spread(kall)
-    hand_on(sall, s_copies)
-
-    def gradients(d):
+        raw[0, h] = piece.astype(BF16)
+        k_copies.append(spread(lambda d, h=h: raw.at[d, h]))
+    hand_on(lambda d: sall.at[d], s_copies)
+
+    def normalise(d):
+        pieces = [raw[d, h].astype(F32) for h in range(heads)]
+        total_sq = jnp.sum(pieces[0] * pieces[0], axis=-1, keepdims=True)
+        for piece in pieces[1:]:
+            total_sq = total_sq + jnp.sum(piece * piece, axis=-1, keepdims=True)
+        norm = lax.rsqrt(total_sq * (1.0 / width) + 1e-06)
+        for hs, piece in zip(spans, pieces):
+            kall[d, :, hs] = (piece * norm).astype(BF16)
+
+    def factors(d):
+        normalise(d)
         first = dot(kall[d], wf[...])
         third = dot(kall[d], wt[...])
         back = dot(sall[d], ws[...], NT)
         sig = jax.nn.sigmoid(first)
         gate = first * sig
         return (
-            dot((back * third * (sig * (1.0 + first * (1.0 - sig)))).astype(BF16), kall[d], TN),
-            dot((back * gate).astype(BF16), kall[d], TN),
-            dot((gate * third).astype(BF16), sall[d], TN),
-        )
-
-    for m, grad in enumerate(gradients(0)):
-        gfull[m] = grad
-    for d in [1] + list(range(2, nr, 2)) + list(range(3, nr, 2)):
+            ((back * third * (sig * (1.0 + first * (1.0 - sig)))).astype(BF16), kall),
+            ((back * gate).astype(BF16), kall),
+            ((gate * third).astype(BF16), sall),
+        )
+
+    order = [0] + straight + list(range(3, nr, 2))
+    g_copies = []
+    for d in order:
         if d == 2:
-            hand_on(kall, k_copies)
+            for h in range(heads):
+                hand_on(lambda e, h=h: raw.at[e, h], k_copies[h])
         if d % 2:
-            k_copies[d].wait_recv()
-            s_copies[d].wait_recv()
-        for m, grad in enumerate(gradients(d)):
-            gfull[m] += grad
-    g_copies = []
-    for m in range(3):
-        for z in range(nz):
-            gsend[z, m] = gfull[m, z * part:(z + 1) * part, :].astype(BF16)
-        for d in range(1, nz):
-            g_copies.append(
-                send(gsend.at[view_peer(d), m], grecv.at[d - 1, m], "view", view_peer(d))
-            )
+            for copies in k_copies + [s_copies]:
+                copies[d].wait_recv()
+        for m, (left, right) in enumerate(factors(d)):
+            grad = dot(left, right[d], TN)
+            if d:
+                grad = gfull[m] + grad
+            gfull[m] = grad
+            if d == order[-1]:
+                for z in range(nz):
+                    gsend[z, m] = grad[z * part:(z + 1) * part].astype(BF16)
+                for e in range(1, nz):
+                    g_copies.append(
+                        send(gsend.at[view_peer(e), m], grecv.at[e - 1, m], "view", view_peer(e))
+                    )
     ss[0, 2:3] = jnp.sum(wtr[0] * wtr[0], axis=0, keepdims=True)
     ss[0, 3:4] = jnp.sum(wtr[1] * wtr[1], axis=0, keepdims=True)
     for copy in c_copies:
@@ -425,7 +435,7 @@
         o_copies[d].wait_recv()
         total = total + orecv[d - 1].astype(F32)
     out_ref[...] = total.astype(BF16)
-    for copies in (s_copies, k_copies, o_copies):
+    for copies in k_copies + [s_copies, o_copies]:
         settle(copies)
 
 
@@ -439,14 +449,14 @@
     hid = width // nr
     part = hid // nz
     edge = HALO * cols
-    copies = 4 + 4 * (nr - 1) + 8 * (nz - 1)
-    smem = pl.BlockSpec(memory_space=pltpu.SMEM)
+    heads = width // ATT_HD
+    copies = 4 + (3 + heads) * (nr - 1) + 8 * (nz - 1)
     anywhere = pl.BlockSpec(memory_space=pl.ANY)
     flat = lambda a: a.reshape(tokens, width)
     out = pl.pallas_call(
         functools.partial(step_kernel, nr, nz, cols),
-        out_shape=jax.ShapeDtypeStruct((tokens, width), BF16),
-        in_specs=[anywhere] * 5 + [smem] * 2 + [anywhere] * 3,
+        out_shape=pltpu.VMEM((tokens, width), BF16),
+        in_specs=[anywhere] * 5 + [pl.BlockSpec(memory_space=pltpu.HBM)] * 2 + [anywhere] * 3,
         out_specs=pl.BlockSpec(memory_space=pltpu.VMEM),
         scratch_shapes=[
             pltpu.VMEM((tokens, width), BF16),
@@ -454,10 +464,13 @@
             pltpu.VMEM((tokens, width), BF16),
             pltpu.VMEM((tokens, width), BF16),
             pltpu.VMEM((1, tokens), F32),
+            pltpu.SMEM((row_count,), jnp.int32),
+            pltpu.SMEM((1,), jnp.int32),
             pltpu.VMEM((width, hid), BF16),
             pltpu.VMEM((width, hid), BF16),
             pltpu.VMEM((hid, width), BF16),
             pltpu.VMEM((2, 2 * edge, width), BF16),
+            pltpu.VMEM((nr, heads, tokens, ATT_HD), BF16),
             pltpu.VMEM((nr, tokens, width), BF16),
             pltpu.VMEM((nr, tokens, width), BF16),
             pltpu.VMEM((nz, 8, 128), F32),
@@ -470,7 +483,7 @@
             pltpu.VMEM((nz, 2, width), F32),
             pltpu.VMEM((nr - 1, tokens, width), BF16),
             pltpu.VMEM((nr - 1, tokens, width), BF16),
-            pltpu.SemaphoreType.DMA((8,)),
+            pltpu.SemaphoreType.DMA((10,)),
             pltpu.SemaphoreType.DMA((copies,)),
             pltpu.SemaphoreType.DMA((copies,)),
         ],

time: 44.8 us -> 42.4 us (0.946)
  Pallas kernels: 42.4 us -> 40.9 us
  local copies, waits for them, and re-layouts: 1.57 us -> 0.66 us
    pallas_call x1, Pallas kernels: 42.4 us -> 40.9 us  [fused_step(): pl.pallas_call(functools.partial(step_kernel, nr, nz, cols), out_shape=pl...]
    unnamed x1, local copies, waits for them, and re-layouts: 1.57 us -> 0.66 us
where the time goes in v3:
time: 42.4 us; the launch traced here: 42.3 us
  Pallas kernels  40.9 us (96%)
  local copies, waits for them, and re-layouts  0.66 us (2%)
  between operations  0.66 us (2%)
    pallas_call x1, Pallas kernels, fused_step(): pl.pallas_call(functools.partial(step_kernel, nr, nz, cols), out_shape=pl...  40.9 us

profile of v3, /device:TPU:0, one launch (start us, length us, event | category | flops | bytes accessed | tf_op | source)
XLA Modules:
  0.0 42.3 jit_solution(18151757731060901439)
XLA Ops:
  0.7 40.9 %shard_map.100 = bf16[128,512]{1,0:T(8,128)(2,1)S(1)} custom-call(bf16[128,512]{1,0:T(8,128)(2,1)} %bitcast.13, bf16[128,512]{1,0:T(8,128)(2,1)} %bitcast.14, bf16[128,512]{1,0:T(8,128)(2,1)} %bitcast.15, bf16[128,512]{1,0:T(8,128)(2,1)} %bitcast.16, f32[1,128]{1,0:T(1,128)} %bitcast.17, s32[8]{0:T(128)} %reach_hbm.1, s32[1]{0:T(128)S(6)} %copy.13.count_hbm, ...), custom_call_target="tpu_custom_call" | custom-call | tf_op jit(solution)/shard_map/pallas_call | solution.py:456
  41.6 0.7 %copy.12 = bf16[1,8,16,512]{3,2,1,0:T(8,128)(2,1)} copy(bf16[1,8,16,512]{3,2,1,0:T(8,128)(2,1)S(1)} %bitcast.9) | data formatting | bytes 262144

commit v4 on v3

--- a/solution.py
+++ b/solution.py
@@ -188,6 +188,7 @@
     out_ref,
     q_ref, k_ref, v_ref, t_ref, rates_ref, reach_ref, count_ref, wf, wt, ws, halo, raw, kall, sall, cnt, gfull, gsend, grecv,
     wtr, news, ss, ssz, osend, orecv, load_sem, send_sem, recv_sem,
+    wsend_sem, wrecv_sem,
 ):
     tokens, width = q_ref.shape
     rows_here = tokens // cols
@@ -195,10 +196,11 @@
     part = hid // nz
     edge = HALO * cols
     heads = width // ATT_HD
+    cuts = [0, part // 2] if part % 32 == 0 else [0]
+    step = part // len(cuts)
     me = lax.axis_index("row")
     mz = lax.axis_index("view")
     mine = pl.ds(pl.multiple_of(me * hid, hid), hid)
-    here = pl.ds(pl.multiple_of(mz * part, part), part)
 
     def view_peer(shift):
         return lax.rem(mz + (shift + nz), nz)
@@ -253,8 +255,8 @@
     tok_base = me * tokens
     for load in loads[:2]:
         load.wait()
-    view_total = count_ref[0]
-    cnt[0] = jnp.full((8, 128), view_total, jnp.int32).astype(F32)
+    view_total = count_ref[...]
+    cnt[0] = jnp.broadcast_to(view_total.astype(F32), (8, 128))
     sub = lax.broadcasted_iota(jnp.int32, (tokens, tokens), 0)
     lane = lax.broadcasted_iota(jnp.int32, (tokens, tokens), 1)
     tok_col = tok_base + lax.broadcasted_iota(jnp.int32, (tokens, 1), 0)
@@ -360,10 +362,15 @@
             if d == order[-1]:
                 for z in range(nz):
                     gsend[z, m] = grad[z * part:(z + 1) * part].astype(BF16)
-                for e in range(1, nz):
-                    g_copies.append(
-                        send(gsend.at[view_peer(e), m], grecv.at[e - 1, m], "view", view_peer(e))
-                    )
+                for off in cuts:
+                    rows = pl.ds(off, step)
+                    g_copies.append([
+                        send(
+                            gsend.at[view_peer(e), m, rows], grecv.at[e - 1, m, rows],
+                            "view", view_peer(e),
+                        )
+                        for e in range(1, nz)
+                    ])
     ss[0, 2:3] = jnp.sum(wtr[0] * wtr[0], axis=0, keepdims=True)
     ss[0, 3:4] = jnp.sum(wtr[1] * wtr[1], axis=0, keepdims=True)
     for copy in c_copies:
@@ -372,14 +379,43 @@
     for d in range(1, nz):
         total_valid = total_valid + cnt[d, 0:1, 0:1]
 
-    w_copies = []
-    for m in range(3):
-        for copy in g_copies[m * (nz - 1):(m + 1) * (nz - 1)]:
+    line = nz == 4
+    side = lax.div(mz, 2)
+    outer = lax.rem(mz, 3) == 0
+    if line:
+        partner = jnp.where(outer, 1 + side, 3 * side)
+        targets = [2 - side, partner]
+        sources = [2 - side, 3 - 3 * side, partner]
+    else:
+        targets = [view_peer(d) for d in range(1, nz)]
+        sources = targets
+
+    def weight_copy(chunk, source, to, way):
+        m, off = divmod(chunk, len(cuts))
+        spot = news.at[source, m, pl.ds(cuts[off], step)]
+        return pltpu.make_async_remote_copy(
+            src_ref=spot, dst_ref=spot,
+            send_sem=wsend_sem.at[chunk, way], recv_sem=wrecv_sem.at[chunk, source],
+            device_id={"view": to}, device_id_type=MESH,
+        )
+
+    def relay(chunk, ways):
+        weight_copy(chunk, sources[ways], sources[ways], 0).wait_recv()
+        if line and ways < 2:
+            @pl.when(jnp.logical_not(outer))
+            def _():
+                weight_copy(chunk, sources[ways], partner, 2 + ways).start()
+
+    def raise_chunk(chunk):
+        m, off = divmod(chunk, len(cuts))
+        off = cuts[off]
+        for copy in g_copies[chunk]:
             copy.wait()
-        grad = gfull[m, here, :]
+        rows = pl.ds(pl.multiple_of(mz * part + off, step), step)
+        grad = gfull[m, rows, :]
         for d in range(1, nz):
-            grad = grad + grecv[d - 1, m].astype(F32)
-        old = wtr[m, here, :]
+            grad = grad + grecv[d - 1, m, off:off + step].astype(F32)
+        old = wtr[m, rows, :]
         raised = old + grad / total_valid
         if m == 2:
             rescale = jnp.sqrt(jnp.sum(old * old, -1, keepdims=True) + 1e-06) / jnp.sqrt(
@@ -387,12 +423,23 @@
             )
             raised = raised * rescale
         else:
-            ss[0, m:m + 1] = jnp.sum(raised * raised, axis=0, keepdims=True)
-        news[0, m] = raised.astype(BF16)
-        for d in range(1, nz):
-            w_copies.append(send(news.at[0, m], news.at[d, m], "view", view_peer(d)))
-        if m == 1:
+            squares = jnp.sum(raised * raised, axis=0, keepdims=True)
+            if off:
+                squares = ss[0, m:m + 1] + squares
+            ss[0, m:m + 1] = squares
+        news[mz, m, off:off + step] = raised.astype(BF16)
+        for way, to in enumerate(targets):
+            weight_copy(chunk, mz, to, way).start()
+
+    chunks = 3 * len(cuts)
+    lag = 2 * len(cuts) - 1
+    for chunk in range(chunks):
+        raise_chunk(chunk)
+        if chunk == 2 * len(cuts) - 1:
             ss_copies = [send(ss.at[0], ss.at[d], "row", flip(me, d)) for d in range(1, nr)]
+        if chunk >= lag:
+            for ways in range(len(sources)):
+                relay(chunk - lag, ways)
     for copy in ss_copies:
         copy.wait()
     strip_sums = ss[0]
@@ -400,6 +447,9 @@
         strip_sums = strip_sums + ss[d]
     ssz[0] = strip_sums[0:2]
     ssz_copies = [send(ssz.at[0], ssz.at[d], "view", view_peer(d)) for d in range(1, nz)]
+    for chunk in range(chunks - lag, chunks):
+        for ways in range(len(sources)):
+            relay(chunk, ways)
     for copy in ssz_copies:
         copy.wait()
     new_sums = ssz[0]
@@ -407,8 +457,6 @@
         new_sums = new_sums + ssz[d]
     scales = jnp.sqrt(strip_sums[2:4] + 1e-06) / jnp.sqrt(new_sums + 1e-06)
 
-    for copy in w_copies:
-        copy.wait()
     new_first, new_third, new_second = (
         jnp.concatenate([news[d, m] for d in range(nz)], axis=0) for m in range(3)
     )
@@ -437,6 +485,15 @@
     out_ref[...] = total.astype(BF16)
     for copies in k_copies + [s_copies, o_copies]:
         settle(copies)
+    for chunk in range(chunks):
+        for way, to in enumerate(targets):
+            weight_copy(chunk, mz, to, way).wait_send()
+    if line:
+        @pl.when(jnp.logical_not(outer))
+        def _():
+            for chunk in range(chunks):
+                for way in range(2):
+                    weight_copy(chunk, sources[way], partner, 2 + way).wait_send()
 
 
 def fused_step(
@@ -450,7 +507,8 @@
     part = hid // nz
     edge = HALO * cols
     heads = width // ATT_HD
-    copies = 4 + (3 + heads) * (nr - 1) + 8 * (nz - 1)
+    cuts = 2 if part % 32 == 0 else 1
+    copies = 4 + (3 + heads) * (nr - 1) + (2 + 3 * cuts) * (nz - 1)
     anywhere = pl.BlockSpec(memory_space=pl.ANY)
     flat = lambda a: a.reshape(tokens, width)
     out = pl.pallas_call(
@@ -465,7 +523,7 @@
             pltpu.VMEM((tokens, width), BF16),
             pltpu.VMEM((1, tokens), F32),
             pltpu.SMEM((row_count,), jnp.int32),
-            pltpu.SMEM((1,), jnp.int32),
+            pltpu.VMEM((1, 1), jnp.int32),
             pltpu.VMEM((width, hid), BF16),
             pltpu.VMEM((width, hid), BF16),
             pltpu.VMEM((hid, width), BF16),
@@ -486,11 +544,13 @@
             pltpu.SemaphoreType.DMA((10,)),
             pltpu.SemaphoreType.DMA((copies,)),
             pltpu.SemaphoreType.DMA((copies,)),
+            pltpu.SemaphoreType.DMA((3 * cuts, max(nz, 4))),
+            pltpu.SemaphoreType.DMA((3 * cuts, nz)),
         ],
         compiler_params=pltpu.CompilerParams(collective_id=0, has_side_effects=True),
     )(
         flat(query_feats), flat(key_feats), flat(value_feats), flat(target),
-        token_rates.reshape(1, tokens), row_reach, view_counts,
+        token_rates.reshape(1, tokens), row_reach, view_counts.reshape(1, 1),
         w_first.reshape(width, width), w_third.reshape(width, width), w_second.reshape(width, width),
     )
     return out.reshape(query_feats.shape)

time: 42.4 us -> 45.2 us (1.066)
  Pallas kernels: 40.9 us -> 43.7 us
    pallas_call x1, Pallas kernels: 40.9 us -> 43.7 us  [fused_step(): pl.pallas_call(functools.partial(step_kernel, nr, nz, cols), out_shape=pl...]
where the time goes in v4:
time: 45.2 us; the launch traced here: 45.1 us
  Pallas kernels  43.7 us (97%)
  local copies, waits for them, and re-layouts  0.66 us (1%)
  between operations  0.66 us (1%)
    pallas_call x1, Pallas kernels, fused_step(): pl.pallas_call(functools.partial(step_kernel, nr, nz, cols), out_shape=pl...  43.7 us

profile of v4, /device:TPU:0, one launch (start us, length us, event | category | flops | bytes accessed | tf_op | source)
XLA Modules:
  0.0 45.1 jit_solution(15301696754058789495)
XLA Ops:
  0.7 43.7 %shard_map.100 = bf16[128,512]{1,0:T(8,128)(2,1)S(1)} custom-call(bf16[128,512]{1,0:T(8,128)(2,1)} %bitcast.15, bf16[128,512]{1,0:T(8,128)(2,1)} %bitcast.16, bf16[128,512]{1,0:T(8,128)(2,1)} %bitcast.17, bf16[128,512]{1,0:T(8,128)(2,1)} %bitcast.18, f32[1,128]{1,0:T(1,128)} %bitcast.19, s32[8]{0:T(128)} %reach_hbm.1, s32[1,1]{1,0:T(1,128)} %bitcast.10.count_hbm, ...), custom_call_target="tpu_custom_call" | custom-call | tf_op jit(solution)/shard_map/pallas_call | solution.py:514
  44.4 0.7 %copy.12 = bf16[1,8,16,512]{3,2,1,0:T(8,128)(2,1)} copy(bf16[1,8,16,512]{3,2,1,0:T(8,128)(2,1)S(1)} %bitcast.11) | data formatting | bytes 262144

commit v5 on v3

--- a/solution.py
+++ b/solution.py
@@ -200,8 +200,8 @@
     mine = pl.ds(pl.multiple_of(me * hid, hid), hid)
     here = pl.ds(pl.multiple_of(mz * part, part), part)
 
-    def view_peer(shift):
-        return lax.rem(mz + (shift + nz), nz)
+    def view_peer(bits):
+        return flip(mz, bits)
 
     barrier = pltpu.get_barrier_semaphore()
     for d in range(1, nr):
@@ -360,7 +360,7 @@
             if d == order[-1]:
                 for z in range(nz):
                     gsend[z, m] = grad[z * part:(z + 1) * part].astype(BF16)
-                for e in range(1, nz):
+                for e in range(nz - 1, 0, -1):
                     g_copies.append(
                         send(gsend.at[view_peer(e), m], grecv.at[e - 1, m], "view", view_peer(e))
                     )
@@ -389,7 +389,7 @@
         else:
             ss[0, m:m + 1] = jnp.sum(raised * raised, axis=0, keepdims=True)
         news[0, m] = raised.astype(BF16)
-        for d in range(1, nz):
+        for d in range(nz - 1, 0, -1):
             w_copies.append(send(news.at[0, m], news.at[d, m], "view", view_peer(d)))
         if m == 1:
             ss_copies = [send(ss.at[0], ss.at[d], "row", flip(me, d)) for d in range(1, nr)]
@@ -511,7 +511,7 @@
     )
     nr, nz = mesh.shape["row"], mesh.shape["view"]
     pairs = nr > 1 and nr & (nr - 1) == 0
-    fits = pairs and nz > 1 and HD % (128 * nr) == 0 and HD % (16 * nr * nz) == 0
+    fits = pairs and nz > 1 and nz & (nz - 1) == 0 and HD % (128 * nr) == 0 and HD % (16 * nr * nz) == 0
     return jax.shard_map(
         functools.partial(fused_step, nr, nz) if fits else per_device,
         mesh=mesh,

time: 42.4 us -> 42.3 us (level)
  no operation moved by 1% of the time
where the time goes in v5:
time: 42.3 us; the launch traced here: 42.1 us
  Pallas kernels  40.8 us (96%)
  local copies, waits for them, and re-layouts  0.66 us (2%)
  between operations  0.66 us (2%)
    pallas_call x1, Pallas kernels, fused_step(): pl.pallas_call(functools.partial(step_kernel, nr, nz, cols), out_shape=pl...  40.8 us

profile of v5, /device:TPU:0, one launch (start us, length us, event | category | flops | bytes accessed | tf_op | source)
XLA Modules:
  0.0 42.1 jit_solution(3961916054291397519)
XLA Ops:
  0.7 40.8 %shard_map.100 = bf16[128,512]{1,0:T(8,128)(2,1)S(1)} custom-call(bf16[128,512]{1,0:T(8,128)(2,1)} %bitcast.13, bf16[128,512]{1,0:T(8,128)(2,1)} %bitcast.14, bf16[128,512]{1,0:T(8,128)(2,1)} %bitcast.15, bf16[128,512]{1,0:T(8,128)(2,1)} %bitcast.16, f32[1,128]{1,0:T(1,128)} %bitcast.17, s32[8]{0:T(128)} %reach_hbm.1, s32[1]{0:T(128)S(6)} %copy.13.count_hbm, ...), custom_call_target="tpu_custom_call" | custom-call | tf_op jit(solution)/shard_map/pallas_call | solution.py:456
  41.5 0.7 %copy.12 = bf16[1,8,16,512]{3,2,1,0:T(8,128)(2,1)} copy(bf16[1,8,16,512]{3,2,1,0:T(8,128)(2,1)S(1)} %bitcast.9) | data formatting | bytes 262144
